TPU v7x, 256 devices: a whole 4x4x8 slice. The times are simulated.
256 devices in a mesh: dp: 2 (over core), pipe: 8 (over y, x_lo), tensor: 16 (over x_hi, z).
Axes of the slice: x: 4 (x_hi: 2, x_lo: 2; x = x_hi * 2 + x_lo), y: 4, z: 8, core: 2. Of those that a mesh axis runs over, the one named last changes fastest.
Arguments:
- forward_acts: bfloat16 [1024, 8192], P(('dp', 'tensor'), 'pipe'), parts along dimension 0, may hold values from -6 to 6
- backward_grad: bfloat16 [1024, 8192], P(('dp', 'tensor'), 'pipe'), parts along dimension 0, may hold values from -6 to 6
- stored_gate: bfloat16 [1024, 14336], P(('dp', 'pipe'), 'tensor'), parts along dimension 0, may hold values from -8 to 8
- stored_up: bfloat16 [1024, 14336], P(('dp', 'pipe'), 'tensor'), parts along dimension 0, may hold values from -6 to 6
- gate_weight: bfloat16 [8192, 14336], P('pipe', 'tensor'), may hold values from -0.0625 to 0.0625
- up_weight: bfloat16 [8192, 14336], P('pipe', 'tensor'), may hold values from -0.0625 to 0.0625
- down_weight: bfloat16 [14336, 8192], P('tensor', 'pipe'), may hold values from -0.046875 to 0.046875
Outputs:
- layer_output: bfloat16 [1024, 8192], P(('dp', 'tensor'), 'pipe'), parts along dimension 0
- input_grad: bfloat16 [1024, 8192], P(('dp', 'tensor'), 'pipe'), parts along dimension 0
There are 2 independent parts, one for each index of `dp`. A program takes and returns all parts, laid end to end along the dimension named above; an argument that names none is the same for every part. Nothing has to cross between parts.
All inputs are finite; a program needn't handle non-finite values.
Results may differ from a plain program's by a relative error of at most 0.005.
Values may be sent and summed in bfloat16 or wider, within the bound.
A program may use at most 64 MiB of HBM per device.

v0:
```python
import jax
import jax.numpy as jnp
from jax import lax
from jax.sharding import PartitionSpec as P


def make_slopes(hidden_grad, gate_vals, up_vals):
    gate_wide = gate_vals.astype(jnp.float32)
    up_wide = up_vals.astype(jnp.float32)
    sigma = jax.nn.sigmoid(gate_wide)
    gate_slope = (hidden_grad * up_wide * sigma * (1.0 + gate_wide * (1.0 - sigma))).astype(
        jnp.bfloat16
    )
    up_slope = (hidden_grad * gate_wide * sigma).astype(jnp.bfloat16)
    return jnp.concatenate([gate_slope, up_slope], axis=1)


def per_device(
    forward_acts, backward_grad, stored_gate, stored_up, gate_weight, up_weight, down_weight
):
    hidden_width = gate_weight.shape[1]
    contract_last = (((1,), (1,)), ((), ()))
    paired = jnp.concatenate([gate_weight, up_weight], axis=1)
    whole_acts = lax.all_gather(forward_acts, "tensor", axis=0, tiled=True)
    picked = whole_acts
    summed = lax.psum_scatter(
        jnp.dot(picked, paired, preferred_element_type=jnp.float32),
        "pipe",
        scatter_dimension=0,
        tiled=True,
    )
    hidden_part = (jax.nn.silu(summed[:, :hidden_width]) * summed[:, hidden_width:]).astype(
        jnp.bfloat16
    )
    hidden = lax.all_gather(hidden_part, "pipe", axis=0, tiled=True)
    picked = hidden
    layer_output = lax.psum_scatter(
        jnp.dot(picked, down_weight, preferred_element_type=jnp.float32),
        "tensor",
        scatter_dimension=0,
        tiled=True,
    ).astype(jnp.bfloat16)
    whole_grad = lax.all_gather(backward_grad, "tensor", axis=0, tiled=True)
    picked = whole_grad
    hidden_grad = lax.psum_scatter(
        lax.dot_general(picked, down_weight, contract_last, preferred_element_type=jnp.float32),
        "pipe",
        scatter_dimension=0,
        tiled=True,
    )
    local_slopes = make_slopes(hidden_grad, stored_gate, stored_up)
    all_slopes = lax.all_gather(local_slopes, "pipe", axis=0, tiled=True)
    picked = all_slopes
    input_grad = lax.psum_scatter(
        lax.dot_general(picked, paired, contract_last, preferred_element_type=jnp.float32),
        "tensor",
        scatter_dimension=0,
        tiled=True,
    ).astype(jnp.bfloat16)
    return (layer_output, input_grad)


def solution(mesh):
    in_specs = (
        P(("dp", "tensor"), "pipe"),
        P(("dp", "tensor"), "pipe"),
        P(("dp", "pipe"), "tensor"),
        P(("dp", "pipe"), "tensor"),
        P("pipe", "tensor"),
        P("pipe", "tensor"),
        P("tensor", "pipe"),
    )
    out_specs = (P(("dp", "tensor"), "pipe"), P(("dp", "tensor"), "pipe"))
    return jax.shard_map(
        per_device, mesh=mesh, in_specs=in_specs, out_specs=out_specs, check_vma=False
    )
```

profile of v0, /device:TPU:8, one launch (start us, length us, event | category | flops | bytes accessed | tf_op | source)
XLA Modules:
  0.0 779.6 jit_solution(1164099196765025358)
XLA Ops:
  7.2 0.0 all-gather.6.cloned.1.call-start
  7.2 0.7 all-gather.6.cloned.1.call-update
  7.9 0.0 reduce-scatter.15.cloned.1.call-start
  8.0 84.3 %all-gather.6.cloned.1.call-done = bf16[512,1024]{1,0:T(8,128)(2,1)} async-done(((bf16[32,1024]{1,0:T(8,128)(2,1)}), bf16[512,1024]{1,0:T(8,128)(2,1)}) %all-gather.6.cloned.1.call-update) | async-done | bytes 1048592 | tf_op jit(solution)/shard_map/all_gather | solution.py:43
  92.3 3.8 fusion.10
  96.1 0.0 all-gather.4.cloned.1.call-start
  96.2 0.7 all-gather.4.cloned.1.call-update
  96.9 0.0 all-gather.8.cloned.1.call-start
  96.9 44.3 %reduce-scatter.15.cloned.1.call-done = f32[64,896]{1,0:T(8,128)} async-done(((f32[512,896]{1,0:T(8,128)}), f32[64,896]{1,0:T(8,128)}) %reduce-scatter.15.cloned.1.call-update) | async-done | bytes 229392 | tf_op jit(solution)/shard_map/reduce_scatter | solution.py:45
  141.2 1.1 fusion.5
  142.3 0.7 pad_maximum_fusion
  143.0 0.0 all-gather.8.cloned.1.call-update
  143.0 0.0 reduce-scatter.13.cloned.1.call-start
  143.1 3.1 constant_dynamic-update-slice_fusion.1
  146.2 1.4 constant_dynamic-update-slice_fusion
  147.6 76.1 %all-gather.4.cloned.1.call-done = bf16[512,1024]{1,0:T(8,128)(2,1)} async-done(((bf16[32,1024]{1,0:T(8,128)(2,1)}), bf16[512,1024]{1,0:T(8,128)(2,1)}) %all-gather.4.cloned.1.call-update) | async-done | bytes 1048592 | tf_op jit(solution)/shard_map/all_gather | solution.py:24
  223.7 6.3 convolution_bitcast_fusion
  230.0 5.1 copy.23
  235.1 0.0 reduce-scatter.13.cloned.1.call-update
  235.1 0.0 reduce-scatter.11.cloned.1.call-start
  235.2 34.7 %all-gather.8.cloned.1.call-done = bf16[512,1792]{1,0:T(8,128)(2,1)} async-done(((bf16[64,1792]{1,0:T(8,128)(2,1)}), bf16[512,1792]{1,0:T(8,128)(2,1)}) %all-gather.8.cloned.1.call-update) | async-done | bytes 1835024 | tf_op jit(solution)/shard_map/all_gather | solution.py:52
  269.9 6.0 fusion.11
  276.0 0.0 reduce-scatter.11.cloned.1.call-update
  276.0 0.0 reduce-scatter.9.cloned.1.call-start
  276.0 80.3 %reduce-scatter.13.cloned.1.call-done = f32[64,1792]{1,0:T(8,128)} async-done(((f32[512,1792]{1,0:T(8,128)}), f32[64,1792]{1,0:T(8,128)}) %reduce-scatter.13.cloned.1.call-update) | async-done | bytes 458768 | tf_op jit(solution)/shard_map/reduce_scatter | solution.py:26
  356.3 1.1 fusion.8
  357.4 30.6 %all_gather.13 = bf16[512,896]{1,0:T(8,128)(2,1)S(1)} all-gather(bf16[64,896]{1,0:T(8,128)(2,1)S(1)} %fusion.8), channel_id=1, replica_groups=mesh['dp'=2,'pipe'=8,'tensor'=16] {'pipe'}, dimensions={0}, use_global_device_ids=true | all-gather | bytes 1032192 | tf_op jit(solution)/shard_map/all_gather | solution.py:35
  388.1 2.6 fusion.9
  390.7 174.5 %reduce-scatter.11.cloned.1.call-done = f32[32,1024]{1,0:T(8,128)} async-done(((f32[512,1024]{1,0:T(8,128)}), f32[32,1024]{1,0:T(8,128)}) %reduce-scatter.11.cloned.1.call-update) | async-done | bytes 131088 | tf_op jit(solution)/shard_map/reduce_scatter | solution.py:54
  565.2 1.5 convert_element_type.27
  566.7 204.5 %reduce-scatter.9.cloned.1.call-done = f32[32,1024]{1,0:T(8,128)} async-done(((f32[512,1024]{1,0:T(8,128)}), f32[32,1024]{1,0:T(8,128)}) %reduce-scatter.9.cloned.1.call-update) | async-done | bytes 131088 | tf_op jit(solution)/shard_map/reduce_scatter | solution.py:37
  771.2 1.5 convert_element_type.22
  (10 shorter events, 0.1 us)
Async XLA Ops:
  7.2 85.2 %copy-start = (bf16[896,1024]{1,0:T(8,128)(2,1)S(1)}, bf16[896,1024]{1,0:T(8,128)(2,1)}, u32[]{:S(2)}) copy-start(bf16[896,1024]{1,0:T(8,128)(2,1)} %param.13) | copy-start | bytes 5505028
  7.2 85.1 %all-gather.6.cloned.1.call-start = ((), (), s32[]{:S(2)}) async-start(), calls=%async_computation.6 | async-start | bytes 1114112 | tf_op jit(solution)/shard_map/all_gather | solution.py:43
  7.9 133.3 %copy-start.2 = (bf16[64,896]{1,0:T(8,128)(2,1)S(1)}, bf16[64,896]{1,0:T(8,128)(2,1)}, u32[]{:S(2)}) copy-start(bf16[64,896]{1,0:T(8,128)(2,1)} %param.9) | copy-start | bytes 344068
  7.9 133.3 %copy-start.3 = (bf16[64,896]{1,0:T(8,128)(2,1)S(1)}, bf16[64,896]{1,0:T(8,128)(2,1)}, u32[]{:S(2)}) copy-start(bf16[64,896]{1,0:T(8,128)(2,1)} %param.10) | copy-start | bytes 344068
  7.9 133.3 %reduce-scatter.15.cloned.1.call-start = ((), (), s32[]{:S(2)}) async-start(), calls=%async_computation.10 | async-start | bytes 2064384 | tf_op jit(solution)/shard_map/reduce_scatter | solution.py:45
  96.1 127.5 %all-gather.4.cloned.1.call-start = ((), (), s32[]{:S(2)}) async-start(), calls=%async_computation.4 | async-start | bytes 1114112 | tf_op jit(solution)/shard_map/all_gather | solution.py:24
  96.9 173.1 %all-gather.8.cloned.1.call-start = ((), (), s32[]{:S(2)}) async-start(), calls=%async_computation.7 | async-start | bytes 2064384 | tf_op jit(solution)/shard_map/all_gather | solution.py:52
  143.0 213.3 %reduce-scatter.13.cloned.1.call-start = ((), (), s32[]{:S(2)}) async-start(), calls=%async_computation.9 | async-start | bytes 4128768 | tf_op jit(solution)/shard_map/reduce_scatter | solution.py:26
  143.1 3.1 copy-start.1
  235.1 330.0 %reduce-scatter.11.cloned.1.call-start = ((), (), s32[]{:S(2)}) async-start(), calls=%async_computation.8 | async-start | bytes 2228224 | tf_op jit(solution)/shard_map/reduce_scatter | solution.py:54
  276.0 495.2 %reduce-scatter.9.cloned.1.call-start = ((), (), s32[]{:S(2)}) async-start(), calls=%async_computation.5 | async-start | bytes 2228224 | tf_op jit(solution)/shard_map/reduce_scatter | solution.py:37
Sparse Core Ops, SparseCore 0:
  10.6 81.6 all-gather.5
  96.3 44.9 reduce-scatter.14
  143.8 79.8 all-gather.3
  225.3 44.5 all-gather.7
  272.3 83.9 reduce-scatter.12
  360.0 205.0 reduce-scatter.10
  569.1 202.0 reduce-scatter.8
where the time goes:
time: 780 us
  waiting for transfers between devices  700 us (90%)
  blocking collectives  30.6 us (4%)
  matrix products  18.7 us (2%)
  between operations  14.2 us (2%)
  local copies, waits for them, and re-layouts  9.66 us (1%)
    reduce_scatter x1, waiting for transfers between devices, per_device(): lax.psum_scatter(jnp.dot(picked, down_weight, preferred_element_type=jnp....  204 us
    reduce_scatter x1, waiting for transfers between devices, per_device(): lax.psum_scatter(lax.dot_general(picked, paired, contract_last, preferred...  174 us
    all_gather x1, waiting for transfers between devices, per_device(): whole_grad = lax.all_gather(backward_grad, 'tensor', axis=0, tiled=True)  84.3 us
    reduce_scatter x1, waiting for transfers between devices, per_device(): lax.psum_scatter(jnp.dot(picked, paired, preferred_element_type=jnp.float...  80.3 us
    all_gather x1, waiting for transfers between devices, per_device(): whole_acts = lax.all_gather(forward_acts, 'tensor', axis=0, tiled=True)  76.1 us
    reduce_scatter x1, waiting for transfers between devices, per_device(): lax.psum_scatter(lax.dot_general(picked, down_weight, contract_last, pref...  44.3 us
    all_gather x1, waiting for transfers between devices, per_device(): all_slopes = lax.all_gather(local_slopes, 'pipe', axis=0, tiled=True)  34.7 us
    all_gather x1, blocking collectives, per_device(): hidden = lax.all_gather(hidden_part, 'pipe', axis=0, tiled=True)  30.6 us
  transfers between devices with their start and end apart: 7, of which 7 were waited for; matrix products, arithmetic and copies ran while one was open for 4% of the time, Pallas kernels for 0%

commit v1 on v0

--- a/solution.py
+++ b/solution.py
@@ -40,7 +40,9 @@
         scatter_dimension=0,
         tiled=True,
     ).astype(jnp.bfloat16)
-    whole_grad = lax.all_gather(backward_grad, "tensor", axis=0, tiled=True)
+    whole_grad = jnp.concatenate(
+        lax.all_to_all(jnp.stack([backward_grad] * lax.axis_size("tensor")), "tensor", 0, 0), axis=0
+    )
     picked = whole_grad
     hidden_grad = lax.psum_scatter(
         lax.dot_general(picked, down_weight, contract_last, preferred_element_type=jnp.float32),

time: 780 us -> 671 us (0.86)
  waiting for transfers between devices: 700 us -> 550 us
  blocking collectives: 30.6 us -> 70.4 us
    all_gather x1 -> x0, waiting for transfers between devices: 84.3 us -> none  [per_device(): whole_grad = lax.all_gather(backward_grad, 'tensor', axis=0, tiled=True)]
    reduce_scatter x1, waiting for transfers between devices: 80.3 us -> 13.7 us  [per_device(): lax.psum_scatter(jnp.dot(picked, paired, preferred_element_type=jnp.float...]
    all_gather x1, waiting for transfers between devices: 34.7 us -> 84.1 us  [per_device(): all_slopes = lax.all_gather(local_slopes, 'pipe', axis=0, tiled=True)]
    all_gather x1, waiting for transfers between devices: 76.1 us -> 28.4 us  [per_device(): whole_acts = lax.all_gather(forward_acts, 'tensor', axis=0, tiled=True)]
    all_to_all x0 -> x1, blocking collectives: none -> 39.3 us  [per_device(): lax.all_to_all(jnp.stack([backward_grad] * lax.axis_size('tensor')), 'ten...]
  transfers between devices with their start and end apart: 7 -> 6, of which waited for: 7 -> 6; matrix products, arithmetic and copies ran while one was open for 4% -> 4% of each run, Pallas kernels for 0% -> 0%
where the time goes in v1:
time: 671 us
  waiting for transfers between devices  550 us (82%)
  blocking collectives  70.4 us (10%)
  matrix products  17.5 us (3%)
  between operations  15.3 us (2%)
  local copies, waits for them, and re-layouts  10.9 us (2%)
    reduce_scatter x1, waiting for transfers between devices, per_device(): lax.psum_scatter(jnp.dot(picked, down_weight, preferred_element_type=jnp....  204 us
    reduce_scatter x1, waiting for transfers between devices, per_device(): lax.psum_scatter(lax.dot_general(picked, paired, contract_last, preferred...  174 us
    all_gather x1, waiting for transfers between devices, per_device(): all_slopes = lax.all_gather(local_slopes, 'pipe', axis=0, tiled=True)  84.1 us
    reduce_scatter x1, waiting for transfers between devices, per_device(): lax.psum_scatter(lax.dot_general(picked, down_weight, contract_last, pref...  45 us
    all_to_all x1, blocking collectives, per_device(): lax.all_to_all(jnp.stack([backward_grad] * lax.axis_size('tensor')), 'ten...  39.3 us
    all_gather x1, blocking collectives, per_device(): hidden = lax.all_gather(hidden_part, 'pipe', axis=0, tiled=True)  31.1 us
    all_gather x1, waiting for transfers between devices, per_device(): whole_acts = lax.all_gather(forward_acts, 'tensor', axis=0, tiled=True)  28.4 us
    reduce_scatter x1, waiting for transfers between devices, per_device(): lax.psum_scatter(jnp.dot(picked, paired, preferred_element_type=jnp.float...  13.7 us
  transfers between devices with their start and end apart: 6, of which 6 were waited for; matrix products, arithmetic and copies ran while one was open for 4% of the time, Pallas kernels for 0%

profile of v1, /device:TPU:8, one launch (start us, length us, event | category | flops | bytes accessed | tf_op | source)
XLA Modules:
  0.0 670.6 jit_solution(11660282268850565930)
XLA Ops:
  8.0 0.0 reduce-scatter.15.cloned.1.call-start
  8.1 1.1 stack.2
  9.1 39.3 %all_to_all.5 = bf16[16,32,1024]{2,1,0:T(8,128)(2,1)S(1)} all-to-all(bf16[16,32,1024]{2,1,0:T(8,128)(2,1)S(1)} %stack.2), channel_id=1, replica_groups=mesh['dp'=2,'pipe'=8,'tensor'=16] {'tensor'}, dimensions={0} | all-to-all | bytes 2097152 | tf_op jit(solution)/shard_map/all_to_all | solution.py:44
  48.4 2.5 fusion.10
  51.0 0.0 reduce-scatter.15.cloned.1.call-update
  51.0 0.0 all-gather.3.cloned.1.call-start
  51.0 0.5 all-gather.3.cloned.1.call-update
  51.6 0.0 all-gather.5.cloned.1.call-start
  51.6 45.0 %reduce-scatter.15.cloned.1.call-done = f32[64,896]{1,0:T(8,128)} async-done(((f32[512,896]{1,0:T(8,128)}), f32[64,896]{1,0:T(8,128)}) %reduce-scatter.15.cloned.1.call-update) | async-done | bytes 229392 | tf_op jit(solution)/shard_map/reduce_scatter | solution.py:47
  96.6 1.1 fusion.5
  97.7 0.7 pad_maximum_fusion
  98.4 0.0 all-gather.5.cloned.1.call-update
  98.4 0.0 reduce-scatter.13.cloned.1.call-start
  98.5 3.1 constant_dynamic-update-slice_fusion.1
  101.6 1.5 constant_dynamic-update-slice_fusion
  103.1 28.4 %all-gather.3.cloned.1.call-done = bf16[512,1024]{1,0:T(8,128)(2,1)} async-done(((bf16[32,1024]{1,0:T(8,128)(2,1)}), bf16[512,1024]{1,0:T(8,128)(2,1)}) %all-gather.3.cloned.1.call-update) | async-done | bytes 1048592 | tf_op jit(solution)/shard_map/all_gather | solution.py:24
  131.6 6.3 convolution_bitcast_fusion
  137.8 5.2 copy.23
  143.0 0.0 reduce-scatter.13.cloned.1.call-update
  143.0 0.0 reduce-scatter.11.cloned.1.call-start
  143.1 84.1 %all-gather.5.cloned.1.call-done = bf16[512,1792]{1,0:T(8,128)(2,1)} async-done(((bf16[64,1792]{1,0:T(8,128)(2,1)}), bf16[512,1792]{1,0:T(8,128)(2,1)}) %all-gather.5.cloned.1.call-update) | async-done | bytes 1835024 | tf_op jit(solution)/shard_map/all_gather | solution.py:54
  227.2 6.0 fusion.11
  233.3 0.0 reduce-scatter.11.cloned.1.call-update
  233.3 0.0 reduce-scatter.9.cloned.1.call-start
  233.4 13.7 %reduce-scatter.13.cloned.1.call-done = f32[64,1792]{1,0:T(8,128)} async-done(((f32[512,1792]{1,0:T(8,128)}), f32[64,1792]{1,0:T(8,128)}) %reduce-scatter.13.cloned.1.call-update) | async-done | bytes 458768 | tf_op jit(solution)/shard_map/reduce_scatter | solution.py:26
  247.1 1.1 fusion.8
  248.2 31.1 %all_gather.10 = bf16[512,896]{1,0:T(8,128)(2,1)S(1)} all-gather(bf16[64,896]{1,0:T(8,128)(2,1)S(1)} %fusion.8), channel_id=1, replica_groups=mesh['dp'=2,'pipe'=8,'tensor'=16] {'pipe'}, dimensions={0}, use_global_device_ids=true | all-gather | bytes 1032192 | tf_op jit(solution)/shard_map/all_gather | solution.py:35
  279.3 2.6 fusion.9
  281.9 174.2 %reduce-scatter.11.cloned.1.call-done = f32[32,1024]{1,0:T(8,128)} async-done(((f32[512,1024]{1,0:T(8,128)}), f32[32,1024]{1,0:T(8,128)}) %reduce-scatter.11.cloned.1.call-update) | async-done | bytes 131088 | tf_op jit(solution)/shard_map/reduce_scatter | solution.py:56
  456.1 1.5 convert_element_type.27
  457.7 204.3 %reduce-scatter.9.cloned.1.call-done = f32[32,1024]{1,0:T(8,128)} async-done(((f32[512,1024]{1,0:T(8,128)}), f32[32,1024]{1,0:T(8,128)}) %reduce-scatter.9.cloned.1.call-update) | async-done | bytes 131088 | tf_op jit(solution)/shard_map/reduce_scatter | solution.py:37
  662.0 1.5 convert_element_type.22
  (9 shorter events, 0.0 us)
Async XLA Ops:
  8.0 40.4 %copy-start = (bf16[896,1024]{1,0:T(8,128)(2,1)S(1)}, bf16[896,1024]{1,0:T(8,128)(2,1)}, u32[]{:S(2)}) copy-start(bf16[896,1024]{1,0:T(8,128)(2,1)} %param.13) | copy-start | bytes 5505028
  8.0 88.6 %reduce-scatter.15.cloned.1.call-start = ((), (), s32[]{:S(2)}) async-start(), calls=%async_computation.10 | async-start | bytes 2064384 | tf_op jit(solution)/shard_map/reduce_scatter | solution.py:47
  48.4 48.2 %copy-start.2 = (bf16[64,896]{1,0:T(8,128)(2,1)S(1)}, bf16[64,896]{1,0:T(8,128)(2,1)}, u32[]{:S(2)}) copy-start(bf16[64,896]{1,0:T(8,128)(2,1)} %param.9) | copy-start | bytes 344068
  48.4 48.2 %copy-start.3 = (bf16[64,896]{1,0:T(8,128)(2,1)S(1)}, bf16[64,896]{1,0:T(8,128)(2,1)}, u32[]{:S(2)}) copy-start(bf16[64,896]{1,0:T(8,128)(2,1)} %param.10) | copy-start | bytes 344068
  51.0 80.6 %all-gather.3.cloned.1.call-start = ((), (), s32[]{:S(2)}) async-start(), calls=%async_computation.5 | async-start | bytes 1114112 | tf_op jit(solution)/shard_map/all_gather | solution.py:24
  51.6 175.7 %all-gather.5.cloned.1.call-start = ((), (), s32[]{:S(2)}) async-start(), calls=%async_computation.7 | async-start | bytes 2064384 | tf_op jit(solution)/shard_map/all_gather | solution.py:54
  98.4 148.7 %reduce-scatter.13.cloned.1.call-start = ((), (), s32[]{:S(2)}) async-start(), calls=%async_computation.9 | async-start | bytes 4128768 | tf_op jit(solution)/shard_map/reduce_scatter | solution.py:26
  98.5 3.1 copy-start.1
  143.0 313.1 %reduce-scatter.11.cloned.1.call-start = ((), (), s32[]{:S(2)}) async-start(), calls=%async_computation.8 | async-start | bytes 2228224 | tf_op jit(solution)/shard_map/reduce_scatter | solution.py:56
  233.3 428.7 %reduce-scatter.9.cloned.1.call-start = ((), (), s32[]{:S(2)}) async-start(), calls=%async_computation.6 | async-start | bytes 2228224 | tf_op jit(solution)/shard_map/reduce_scatter | solution.py:37
Sparse Core Ops, SparseCore 0:
  51.1 45.4 reduce-scatter.14
  143.2 103.8 reduce-scatter.12
  251.0 205.1 reduce-scatter.10
  459.9 202.0 reduce-scatter.8
Sparse Core Ops, SparseCore 1:
  54.0 77.5 all-gather.2
  133.2 94.0 all-gather.4
